TPU v7x, 32 devices: a whole 2x2x4 slice. The times are simulated.
32 devices in a mesh: expert: 8 (over z, x), replica: 4 (over y, core).
Axes of the slice: x: 2, y: 2, z: 4, core: 2. Of those that a mesh axis runs over, the one named last changes fastest.
Arguments:
- tokens: bfloat16 [4096, 2048], P(('expert', 'replica')), may hold values from -6 to 6
- cotangent: bfloat16 [4096, 2048], P(('expert', 'replica')), may hold values from -6 to 6
- route_weights: float32 [4096, 8], P(('expert', 'replica')), may hold values from 0.02 to 0.4
- expert_ids: int32 [4096, 8], P(('expert', 'replica')), may hold values from 0 to 15, as said below
- slot_ids: int32 [4096, 8], P(('expert', 'replica')), may hold values from 0 to 63, as said below
- kept_mask: int32 [4096, 8], P(('expert', 'replica')), may hold values from 0 to 1, as said below
- gate_weight: bfloat16 [16, 2048, 384], P('expert'), may hold values from -0.125 to 0.125
- up_weight: bfloat16 [16, 2048, 384], P('expert'), may hold values from -0.125 to 0.125
- down_weight: bfloat16 [16, 384, 2048], P('expert'), may hold values from -0.3125 to 0.3125
- projector_basis: float32 [2048, 256], P('expert'), may hold values from -6 to 6
Outputs:
- token_grads: bfloat16 [4096, 2048], P(('expert', 'replica'))
- projected_grads: float32 [16, 3, 384, 256], P('expert')
- new_basis: float32 [2048, 256], P('expert')
Inputs may be any that keep to these rules, and one draw needn't show every extreme that they name: `expert_ids`: each row names 8 different experts. `slot_ids`: within one device's rows, the kept routes to one expert take slots 0, 1, 2, ... in the order of rows and then of the position in the row; a dropped route has slot 0; in every draw some expert receives 64 kept routes from every device's rows. `kept_mask`: a route is dropped exactly when 64 earlier routes of the same device's rows go to the same expert.
All inputs are finite; a program needn't handle non-finite values.
Results may differ from a plain program's by a relative error of at most 0.019.
Values may be sent and summed in bfloat16 or wider, within the bound.
A program may use at most 128 MiB of HBM per device.

v0:
```python
import math
import jax
import jax.numpy as jnp
from jax import lax
from jax.sharding import PartitionSpec as P


def body(
    tokens,
    cotangent,
    route_weights,
    expert_ids,
    slot_ids,
    kept_mask,
    gate_weight,
    up_weight,
    down_weight,
    projector_basis,
):
    tok_count, model_width = tokens.shape
    route_top = expert_ids.shape[1]
    local_count = gate_weight.shape[0]
    group_count = lax.axis_size("expert")
    expert_total = local_count * group_count
    slot_cap = tok_count * route_top // expert_total
    slot_total = expert_total * slot_cap
    route_count = tok_count * route_top
    target = jnp.where(kept_mask > 0, expert_ids * slot_cap + slot_ids, slot_total).reshape(-1)
    table = (
        jnp.full((slot_total,), route_count, jnp.int32)
        .at[target]
        .set(jnp.arange(route_count, dtype=jnp.int32), mode="drop")
    )
    owner = table // route_top
    tokens_pad = jnp.concatenate([tokens, jnp.zeros((1, model_width), tokens.dtype)], 0)
    cotangent_pad = jnp.concatenate([cotangent, jnp.zeros((1, model_width), cotangent.dtype)], 0)
    weight_pad = jnp.concatenate([route_weights.reshape(-1), jnp.zeros((1,), jnp.float32)], 0)
    x_send = tokens_pad[owner].reshape(group_count, local_count * slot_cap, model_width)
    dy_send = (cotangent_pad[owner].astype(jnp.float32) * weight_pad[table][:, None]).astype(
        jnp.bfloat16
    )
    dy_send = dy_send.reshape(group_count, local_count * slot_cap, model_width)
    full_basis = lax.all_gather(
        projector_basis.astype(jnp.bfloat16), "expert", axis=0, tiled=True
    ).astype(projector_basis.dtype)
    projector = (full_basis * (1.0 / math.sqrt(model_width))).astype(jnp.bfloat16)
    block_shape = (group_count, local_count, slot_cap, model_width)
    x_recv, dy_recv = (
        lax.all_to_all(x_send, "expert", split_axis=0, concat_axis=0, tiled=True),
        lax.all_to_all(dy_send, "expert", split_axis=0, concat_axis=0, tiled=True),
    )
    x_rows = x_recv.reshape(block_shape)
    gate = jnp.einsum("sjcd,jdf->sjcf", x_rows, gate_weight, preferred_element_type=jnp.float32)
    upper = jnp.einsum("sjcd,jdf->sjcf", x_rows, up_weight, preferred_element_type=jnp.float32)
    sigma = jax.nn.sigmoid(gate)
    activated = gate * sigma
    slope = sigma * (1.0 + gate * (1.0 - sigma))
    hidden = (activated * upper).astype(jnp.bfloat16)
    x_proj = jnp.einsum(
        "sjcd,dr->sjcr", x_rows, projector, preferred_element_type=jnp.float32
    ).astype(jnp.bfloat16)
    x_rows, upper, activated, slope, hidden, x_proj = (
        x_rows,
        upper,
        activated,
        slope,
        hidden,
        x_proj,
    )
    dy_rows = dy_recv.reshape(block_shape)
    hidden_grad = jnp.einsum(
        "sjcd,jfd->sjcf", dy_rows, down_weight, preferred_element_type=jnp.float32
    )
    up_grad = (hidden_grad * activated).astype(jnp.bfloat16)
    gate_grad = (hidden_grad * upper * slope).astype(jnp.bfloat16)
    row_grads = jnp.einsum(
        "sjcf,jdf->sjcd", gate_grad, gate_weight, preferred_element_type=jnp.float32
    )
    row_grads = row_grads + jnp.einsum(
        "sjcf,jdf->sjcd", up_grad, up_weight, preferred_element_type=jnp.float32
    )
    row_grads = row_grads.astype(jnp.bfloat16).reshape(
        group_count, local_count * slot_cap, model_width
    )
    returned = lax.all_to_all(row_grads, "expert", split_axis=0, concat_axis=0, tiled=True).reshape(
        slot_total, model_width
    )
    returned = jnp.concatenate([returned, jnp.zeros((1, model_width), jnp.bfloat16)], 0)
    token_grads = jnp.sum(
        returned[target].reshape(tok_count, route_top, model_width).astype(jnp.float32), axis=1
    ).astype(jnp.bfloat16)
    dy_proj = jnp.einsum(
        "sjcd,dr->sjcr", dy_rows, projector, preferred_element_type=jnp.float32
    ).astype(jnp.bfloat16)
    partial_grads = jnp.stack(
        [
            jnp.einsum("sjcf,sjcr->jfr", gate_grad, x_proj, preferred_element_type=jnp.float32),
            jnp.einsum("sjcf,sjcr->jfr", up_grad, x_proj, preferred_element_type=jnp.float32),
            jnp.einsum("sjcf,sjcr->jfr", hidden, dy_proj, preferred_element_type=jnp.float32),
        ],
        1,
    )
    projected_grads = lax.psum(partial_grads, "replica")
    grads_low = projected_grads.astype(jnp.bfloat16)
    mixed = jnp.einsum(
        "sjcf,jfr->sjcr", gate_grad, grads_low[:, 0], preferred_element_type=jnp.float32
    )
    mixed = (
        mixed
        + jnp.einsum("sjcf,jfr->sjcr", up_grad, grads_low[:, 1], preferred_element_type=jnp.float32)
    ).astype(jnp.bfloat16)
    down_mix = jnp.einsum(
        "sjcf,jfr->sjcr", hidden, grads_low[:, 2], preferred_element_type=jnp.float32
    ).astype(jnp.bfloat16)
    power = jnp.einsum("sjcd,sjcr->dr", x_rows, mixed, preferred_element_type=jnp.float32)
    power = power + jnp.einsum(
        "sjcd,sjcr->dr", dy_rows, down_mix, preferred_element_type=jnp.float32
    )
    panel_rows = model_width // group_count
    power_sum = lax.psum(power, ("expert", "replica"))
    gram_total = jnp.dot(
        power_sum.T, power_sum, precision=lax.Precision.HIGHEST, preferred_element_type=jnp.float32
    )
    own_panel = lax.dynamic_slice_in_dim(
        power_sum, lax.axis_index("expert") * panel_rows, panel_rows, 0
    )
    lower = jnp.linalg.cholesky(gram_total)
    new_basis = (
        math.sqrt(model_width) * jax.scipy.linalg.solve_triangular(lower, own_panel.T, lower=True).T
    )
    return (token_grads, projected_grads, new_basis)


def solution(mesh):
    return jax.shard_map(
        body,
        mesh=mesh,
        in_specs=(
            P(("expert", "replica"), None),
            P(("expert", "replica"), None),
            P(("expert", "replica"), None),
            P(("expert", "replica"), None),
            P(("expert", "replica"), None),
            P(("expert", "replica"), None),
            P("expert", None, None),
            P("expert", None, None),
            P("expert", None, None),
            P("expert", None),
        ),
        out_specs=(
            P(("expert", "replica"), None),
            P("expert", None, None, None),
            P("expert", None),
        ),
        check_vma=False,
    )
```

profile of v0, /device:TPU:0, one launch (start us, length us, event | category | flops | bytes accessed | tf_op | source)
XLA Modules:
  0.0 595.4 jit_solution(13270312014699253039)
XLA Ops:
  7.2 0.9 add_select_fusion.2
  8.3 4.3 scatter_custom_fusion
  12.6 0.8 copy.20
  13.5 1.9 concatenate.15
  15.4 10.0 %gather_fusion = bf16[1024,2048]{1,0:T(8,128)(2,1)} fusion(bf16[129,2048]{1,0:T(8,128)(2,1)} %concatenate.15, s32[1024]{0:T(1024)S(1)} %get-tuple-element.37), kind=kCustom, calls=%fused_computation | custom fusion | bytes 8392704 | tf_op jit(solution)/shard_map/gather | solution.py:39
  25.4 6.1 %gather_fusion.1 = f32[1024]{0:T(1024)S(1)} fusion(f32[1025]{0:T(1024)S(1)} %pad_maximum_fusion.1, s32[1024]{0:T(1024)S(1)} %get-tuple-element.36), kind=kCustom, calls=%fused_computation.1 | custom fusion | bytes 12288 | tf_op jit(solution)/shard_map/gather | solution.py:39
  31.5 4.9 fusion
  36.4 7.3 %all-to-all-start = ((bf16[8,128,2048]{2,1,0:T(8,128)(2,1)}), bf16[8,128,2048]{2,1,0:T(8,128)(2,1)}, u32[]{:S(2)}, u32[]{:S(2)}) async-start(bf16[8,128,2048]{2,1,0:T(8,128)(2,1)} %fusion), calls=%async_computation | async-start | bytes 8388608 | tf_op jit(solution)/shard_map/all_to_all | solution.py:50
  43.7 1.9 concatenate.17
  45.6 10.0 %gather_fusion.2 = bf16[1024,2048]{1,0:T(8,128)(2,1)} fusion(bf16[129,2048]{1,0:T(8,128)(2,1)} %concatenate.17, s32[1024]{0:T(1024)S(1)} %get-tuple-element.37), kind=kCustom, calls=%fused_computation.2 | custom fusion | bytes 8392704 | tf_op jit(solution)/shard_map/gather | solution.py:38
  55.6 81.4 %all-to-all-done = bf16[8,128,2048]{2,1,0:T(8,128)(2,1)} async-done(((bf16[8,128,2048]{2,1,0:T(8,128)(2,1)}), bf16[8,128,2048]{2,1,0:T(8,128)(2,1)}, u32[]{:S(2)}, u32[]{:S(2)}) %all-to-all-start) | async-done | bytes 4194336 | tf_op jit(solution)/shard_map/all_to_all | solution.py:50
  137.0 4.7 all-to-all-start.1
  142.3 0.7 convert_element_type.65
  143.0 6.6 %fusion.12 = f32[2,8,64,384]{3,2,1,0:T(8,128)} fusion(bf16[8,2,64,2048]{3,2,1,0:T(8,128)(2,1)} %bitcast.3, bf16[2,384,2048]{2,1,0:T(8,128)(2,1)} %param.18), kind=kOutput, calls=%fused_computation.22 | convolution fusion | flops 1610612736 | bytes 8912896 | tf_op jit(solution)/shard_map/sjcd,jfd->sjcf/dot_general | solution.py:71
  149.6 97.3 %all-to-all-done.1 = bf16[8,128,2048]{2,1,0:T(8,128)(2,1)} async-done(((bf16[8,128,2048]{2,1,0:T(8,128)(2,1)}), bf16[8,128,2048]{2,1,0:T(8,128)(2,1)}, u32[]{:S(2)}, u32[]{:S(2)}) %all-to-all-start.1) | async-done | bytes 4194336 | tf_op jit(solution)/shard_map/all_to_all | solution.py:49
  246.9 5.6 fusion.4
  252.6 6.3 %fusion.36 = (bf16[8,2,64,384]{3,2,0,1:T(8,128)(2,1)}, bf16[8,2,64,384]{3,2,0,1:T(8,128)(2,1)S(1)}, bf16[8,2,64,384]{3,2,0,1:T(8,128)(2,1)}) fusion(f32[2,8,64,384]{3,2,1,0:T(8,128)S(1)} %fusion.4, f32[2,8,64,384]{3,2,1,0:T(8,128)S(1)} %copy-done.13, bf16[2,2048,384]{2,1,0:T(8,128)(2,1)S(1)} %copy-done, bf16[8,2,64,2048]{3,2,1,0:T(8,128)(2,1)} %bitcast.8), kind=kOutput, calls=%fused_computation.47 | convolution fusion | flops 1616510976 | bytes 12845056 | tf_op jit(solution)/shard_map/sjcd,jdf->sjcf/dot_general | solution.py:54
  258.9 0.9 copy-done.4
  259.8 5.6 fusion.14
  265.4 3.9 convolution_convert_fusion.1
  269.3 2.7 convolution_bitcast_fusion.2
  272.0 1.3 convolution_bitcast_fusion.1
  273.4 2.4 fusion.1
  275.8 2.5 copy.24
  278.3 4.7 all-to-all-start.2
  283.1 4.4 convolution_bitcast_fusion
  287.5 1.7 pad_maximum_fusion
  289.4 56.9 %all-reduce.7.cloned.1.call-done = f32[2,3,384,256]{3,2,0,1:T(8,128)} async-done(((f32[2,3,384,256]{3,2,0,1:T(8,128)}), f32[2,3,384,256]{3,2,0,1:T(8,128)}) %all-reduce.7.cloned.1.call-update) | async-done | bytes 2359312 | tf_op jit(solution)/shard_map/psum | solution.py:103
  346.4 1.8 convert_element_type.71
  348.2 1.4 fusion.52
  349.6 5.4 fusion.20
  355.0 6.4 %fusion.26 = f32[2048,256]{1,0:T(8,128)} fusion(f32[2048,256]{1,0:T(8,128)} %fusion.20, bf16[8,2,64,2048]{3,2,1,0:T(8,128)(2,1)} %bitcast.8, f32[2,256,8,64]{1,3,2,0:T(8,128)} %fusion.52, bf16[8,2,64,384]{3,2,0,1:T(8,128)(2,1)S(1)} %copy-done.9, bf16[2,3,384,256]{3,2,0,1:T(8,128)(2,1)} %copy-done.7), kind=kOutput, calls=%fused_computation.32 | convolution fusion | flops 1276116992 | bytes 10616832 | tf_op jit(solution)/shard_map/sjcd,sjcr->dr/dot_general | solution.py:115
  361.5 1.7 copy.30
  363.2 134.4 %all-reduce.9.cloned.1.call-done = f32[2048,256]{1,0:T(8,128)} async-done(((f32[2048,256]{1,0:T(8,128)}), f32[2048,256]{1,0:T(8,128)}) %all-reduce.9.cloned.1.call-update) | async-done | bytes 2097168 | tf_op jit(solution)/shard_map/psum | solution.py:120
  497.6 5.7 fusion.72
  503.5 11.7 %cholesky.50 = f32[128,128]{1,0:T(8,128)S(1)} custom-call(f32[128,128]{1,0:T(8,128)S(1)} %cholesky.118), custom_call_target="Cholesky" | custom-call | tf_op jit(solution)/shard_map/jit(cholesky)/cholesky | solution.py:127
  515.3 10.0 %custom-call.15 = f32[1,128,128]{1,2,0:T(8,128)S(1)} custom-call(f32[1,128,128]{2,1,0:T(8,128)S(1)} %get-tuple-element.33), custom_call_target="InvertDiagBlocksLowerTriangular" | custom-call | tf_op jit(solution)/shard_map/jit(cholesky)/cholesky | solution.py:127
  525.8 11.7 %cholesky.105 = f32[128,128]{1,0:T(8,128)S(1)} custom-call(f32[128,128]{1,0:T(8,128)S(1)} %convolution_subtract_fusion.1), custom_call_target="Cholesky" | custom-call | tf_op jit(solution)/shard_map/jit(cholesky)/cholesky | solution.py:127
  537.5 0.7 compare_reduce_fusion
  539.7 4.1 while.1
  540.3 1.4 bitcast_dynamic-update-slice_fusion.2
  542.3 1.4 bitcast_dynamic-update-slice_fusion.2
  543.7 19.7 %custom-call.16 = f32[2,128,128]{1,2,0:T(8,128)S(1)} custom-call(f32[2,128,128]{2,1,0:T(8,128)S(1)} %get-tuple-element.10), custom_call_target="InvertDiagBlocksLowerTriangular" | custom-call | tf_op jit(solution)/shard_map/jit(_solve_triangular)/triangular_solve | solution.py:129
  563.4 1.0 dynamic-slice_bitcast_fusion
  565.5 0.8 copy.31
  566.3 4.8 concatenate.18
  571.1 11.7 %gather_fusion.3 = bf16[1024,2048]{1,0:T(8,128)(2,1)} fusion(bf16[1025,2048]{1,0:T(8,128)(2,1)} %concatenate.18, s32[1024]{0:T(1024)S(1)} %broadcast_clamp_fusion), kind=kCustom, calls=%fused_computation.3 | custom fusion | bytes 8392704 | tf_op jit(solution)/shard_map/gather | solution.py:90
  582.8 5.9 bitcast_reduce_fusion
  (65 shorter events, 4.3 us)
Async XLA Ops:
  7.2 245.4 %copy-start = (bf16[2,2048,384]{2,1,0:T(8,128)(2,1)S(1)}, bf16[2,2048,384]{2,1,0:T(8,128)(2,1)}, u32[]{:S(2)}) copy-start(bf16[2,2048,384]{2,1,0:T(8,128)(2,1)} %param.17) | copy-start | bytes 9437188
  36.4 100.6 %all-to-all-start = ((bf16[8,128,2048]{2,1,0:T(8,128)(2,1)}), bf16[8,128,2048]{2,1,0:T(8,128)(2,1)}, u32[]{:S(2)}, u32[]{:S(2)}) async-start(bf16[8,128,2048]{2,1,0:T(8,128)(2,1)} %fusion), calls=%async_computation | async-start | bytes 8388608 | tf_op jit(solution)/shard_map/all_to_all | solution.py:50
  137.0 5.2 copy-start.12
  137.0 109.9 %all-to-all-start.1 = ((bf16[8,128,2048]{2,1,0:T(8,128)(2,1)}), bf16[8,128,2048]{2,1,0:T(8,128)(2,1)}, u32[]{:S(2)}, u32[]{:S(2)}) async-start(bf16[8,128,2048]{2,1,0:T(8,128)(2,1)} %bitcast.178), calls=%async_computation.1 | async-start | bytes 8388608 | tf_op jit(solution)/shard_map/all_to_all | solution.py:49
  141.7 123.7 %all-gather.2.cloned.1.call-start = ((), (), s32[]{:S(2)}) async-start(), calls=%async_computation.3 | async-start | bytes 1179648 | tf_op jit(solution)/shard_map/all_gather | solution.py:43
  246.9 5.6 copy-start.13
  252.6 7.2 %copy-start.6 = (bf16[2,2048,384]{2,1,0:T(8,128)(2,1)S(1)}, bf16[2,2048,384]{2,1,0:T(8,128)(2,1)}, u32[]{:S(2)}) copy-start(bf16[2,2048,384]{2,1,0:T(8,128)(2,1)} %param.16) | copy-start | bytes 9437188
  258.9 0.9 copy-start.4
  265.4 6.6 %copy-start.8 = (bf16[8,2,64,384]{3,2,0,1:T(8,128)(2,1)S(1)}, bf16[8,2,64,384]{3,2,0,1:T(8,128)(2,1)}, u32[]{:S(2)}) copy-start(bf16[8,2,64,384]{3,2,0,1:T(8,128)(2,1)} %get-tuple-element.29) | copy-start | bytes 2359300
  265.4 8.0 %copy-start.2 = (f32[2,8,64,2048]{3,2,1,0:T(8,128)S(1)}, f32[2,8,64,2048]{3,2,1,0:T(8,128)}, u32[]{:S(2)}) copy-start(f32[2,8,64,2048]{3,2,1,0:T(8,128)} %fusion.14) | copy-start | bytes 25165828
  278.3 4.7 copy-start.14
  278.3 288.0 %all-to-all-start.2 = ((bf16[8,128,2048]{2,1,0:T(8,128)(2,1)}), bf16[8,128,2048]{2,1,0:T(8,128)(2,1)}, u32[]{:S(2)}, u32[]{:S(2)}) async-start(bf16[8,128,2048]{2,1,0:T(8,128)(2,1)} %bitcast.180), calls=%async_computation.2 | async-start | bytes 8388608 | tf_op jit(solution)/shard_map/all_to_all | solution.py:85
  283.0 63.4 %all-reduce.7.cloned.1.call-start = ((), (), s32[]{:S(2)}) async-start(), calls=%async_computation.4 | async-start | bytes 4718592 | tf_op jit(solution)/shard_map/psum | solution.py:103
  283.0 4.4 copy-start.10
  283.1 4.4 copy-start.11
  289.2 59.0 %copy-start.5 = (bf16[8,2,64,384]{3,2,0,1:T(8,128)(2,1)S(1)}, bf16[8,2,64,384]{3,2,0,1:T(8,128)(2,1)}, u32[]{:S(2)}) copy-start(bf16[8,2,64,384]{3,2,0,1:T(8,128)(2,1)} %copy-done.4) | copy-start | bytes 2359300
  289.2 208.4 %all-reduce.9.cloned.1.call-start = ((), (), s32[]{:S(2)}) async-start(), calls=%async_computation.5 | async-start | bytes 4194304 | tf_op jit(solution)/shard_map/psum | solution.py:120
  348.2 1.5 copy-start.7
  349.6 5.4 copy-start.9
  355.0 6.5 %copy-start.3 = (f32[2,3,384,256]{3,2,0,1:T(8,128)S(1)}, f32[2,3,384,256]{3,2,0,1:T(8,128)}, u32[]{:S(2)}) copy-start(f32[2,3,384,256]{3,2,0,1:T(8,128)} %all-reduce.7.cloned.1.call-done) | copy-start | bytes 7077892
  571.1 17.6 %copy-start.1 = (bf16[2,2048,384]{2,1,0:T(8,128)(2,1)S(1)}, bf16[2,2048,384]{2,1,0:T(8,128)(2,1)}, u32[]{:S(2)}) copy-start(bf16[2,2048,384]{2,1,0:T(8,128)(2,1)} %param.17) | copy-start | bytes 9437188
Sparse Core Ops, SparseCore 0:
  145.2 102.1 all-gather.1
  289.3 56.9 all-reduce.6
  361.6 135.9 all-reduce.8
where the time goes:
time: 600 us; the launch traced here: 595 us
  waiting for transfers between devices  370 us (62%)
  other arithmetic  69.8 us (12%)
  local copies, waits for them, and re-layouts  63 us (10%)
  matrix products  59.4 us (10%)
  starting transfers between devices  17.4 us (3%)
  between operations  15.7 us (3%)
    psum x1, waiting for transfers between devices, body(): power_sum = lax.psum(power, ('expert', 'replica'))  134 us
    all_to_all x1, waiting for transfers between devices, body(): lax.all_to_all(x_send, 'expert', split_axis=0, concat_axis=0, tiled=True)  97.3 us
    all_to_all x1, waiting for transfers between devices, body(): lax.all_to_all(dy_send, 'expert', split_axis=0, concat_axis=0, tiled=True)  81.4 us
    psum x1, waiting for transfers between devices, body(): projected_grads = lax.psum(partial_grads, 'replica')  56.9 us
    another operation x6, other arithmetic, body(): lower = jnp.linalg.cholesky(gram_total)  34.2 us
    another operation x3, other arithmetic, body(): jax.scipy.linalg.solve_triangular(lower, own_panel.T, lower=True)  19.7 us
  transfers between devices with their start and end apart: 6, of which 4 were waited for; matrix products, arithmetic and copies ran while one was open for 21% of the time, Pallas kernels for 0%

commit v1 on v0

--- a/solution.py
+++ b/solution.py
@@ -1,8 +1,16 @@
+import functools
 import math
 import jax
 import jax.numpy as jnp
 from jax import lax
 from jax.sharding import PartitionSpec as P
+
+
+def _put_strips_all(local_values, across):
+    return jnp.sum(lax.all_gather(local_values, axis_name=across), axis=0)
+
+
+plan_trees_now = functools.partial(_put_strips_all, across=("expert", "replica"))
 
 
 def body(
@@ -117,7 +125,7 @@
         "sjcd,sjcr->dr", dy_rows, down_mix, preferred_element_type=jnp.float32
     )
     panel_rows = model_width // group_count
-    power_sum = lax.psum(power, ("expert", "replica"))
+    power_sum = plan_trees_now(power)
     gram_total = jnp.dot(
         power_sum.T, power_sum, precision=lax.Precision.HIGHEST, preferred_element_type=jnp.float32
     )

time: 600 us -> 883 us (1.47)
  waiting for transfers between devices: 370 us -> 617 us
  other arithmetic: 69.8 us -> 97.6 us
    all_gather x0 -> x1, waiting for transfers between devices: none -> 204 us  [_put_strips_all(): return jnp.sum(lax.all_gather(local_values, axis_name=across), axis=0)]
    all_to_all x1, waiting for transfers between devices: 0.01 us -> 191 us  [body(): lax.all_to_all(row_grads, 'expert', split_axis=0, concat_axis=0, tiled=True)]
    psum x1 -> x0, waiting for transfers between devices: 134 us -> none  [body(): power_sum = lax.psum(power, ('expert', 'replica'))]
    all_to_all x1, waiting for transfers between devices: 97.3 us -> 70.1 us  [body(): lax.all_to_all(x_send, 'expert', split_axis=0, concat_axis=0, tiled=True)]
    reduce_sum x0 -> x1, other arithmetic: none -> 22.4 us  [_put_strips_all(): return jnp.sum(lax.all_gather(local_values, axis_name=across), axis=0)]
    all_to_all x1, waiting for transfers between devices: 81.4 us -> 97.3 us  [body(): lax.all_to_all(dy_send, 'expert', split_axis=0, concat_axis=0, tiled=True)]
  transfers between devices with their start and end apart: 6 -> 6, of which waited for: 4 -> 5; matrix products, arithmetic and copies ran while one was open for 21% -> 9% of each run, Pallas kernels for 0% -> 0%
where the time goes in v1:
time: 883 us; the launch traced here: 878 us
  waiting for transfers between devices  617 us (70%)
  other arithmetic  97.6 us (11%)
  local copies, waits for them, and re-layouts  66.6 us (8%)
  matrix products  62.8 us (7%)
  starting transfers between devices  18.2 us (2%)
  between operations  15.5 us (2%)
    all_gather x1, waiting for transfers between devices, _put_strips_all(): return jnp.sum(lax.all_gather(local_values, axis_name=across), axis=0)  204 us
    all_to_all x1, waiting for transfers between devices, body(): lax.all_to_all(row_grads, 'expert', split_axis=0, concat_axis=0, tiled=True)  191 us
    all_to_all x1, waiting for transfers between devices, body(): lax.all_to_all(dy_send, 'expert', split_axis=0, concat_axis=0, tiled=True)  97.3 us
    all_to_all x1, waiting for transfers between devices, body(): lax.all_to_all(x_send, 'expert', split_axis=0, concat_axis=0, tiled=True)  70.1 us
    psum x1, waiting for transfers between devices, body(): projected_grads = lax.psum(partial_grads, 'replica')  54.6 us
    another operation x6, other arithmetic, body(): lower = jnp.linalg.cholesky(gram_total)  34.2 us
    reduce_sum x1, other arithmetic, _put_strips_all(): return jnp.sum(lax.all_gather(local_values, axis_name=across), axis=0)  22.4 us
    another operation x3, other arithmetic, body(): jax.scipy.linalg.solve_triangular(lower, own_panel.T, lower=True)  21.5 us
  transfers between devices with their start and end apart: 6, of which 5 were waited for; matrix products, arithmetic and copies ran while one was open for 9% of the time, Pallas kernels for 0%

profile of v1, /device:TPU:0, one launch (start us, length us, event | category | flops | bytes accessed | tf_op | source)
XLA Modules:
  0.0 878.0 jit_solution(3629382021930836518)
XLA Ops:
  8.3 4.3 scatter_custom_fusion
  12.6 1.9 concatenate.17
  14.5 10.0 %gather_fusion.2 = bf16[1024,2048]{1,0:T(8,128)(2,1)} fusion(bf16[129,2048]{1,0:T(8,128)(2,1)} %concatenate.17, s32[1024]{0:T(1024)S(1)} %get-tuple-element.37), kind=kCustom, calls=%fused_computation.2 | custom fusion | bytes 8392704 | tf_op jit(solution)/shard_map/gather | solution.py:46
  24.5 7.3 all-to-all-start.1
  31.8 1.9 concatenate.15
  33.7 10.0 %gather_fusion = bf16[1024,2048]{1,0:T(8,128)(2,1)} fusion(bf16[129,2048]{1,0:T(8,128)(2,1)} %concatenate.15, s32[1024]{0:T(1024)S(1)} %get-tuple-element.37), kind=kCustom, calls=%fused_computation | custom fusion | bytes 8392704 | tf_op jit(solution)/shard_map/gather | solution.py:47
  43.9 6.2 gather_fusion.1
  50.0 4.9 fusion
  54.9 70.1 %all-to-all-done.1 = bf16[8,128,2048]{2,1,0:T(8,128)(2,1)} async-done(((bf16[8,128,2048]{2,1,0:T(8,128)(2,1)}), bf16[8,128,2048]{2,1,0:T(8,128)(2,1)}, u32[]{:S(2)}, u32[]{:S(2)}) %all-to-all-start.1) | async-done | bytes 4194336 | tf_op jit(solution)/shard_map/all_to_all | solution.py:57
  125.1 4.6 all-to-all-start
  131.0 6.6 fusion.4
  137.6 97.3 %all-to-all-done = bf16[8,128,2048]{2,1,0:T(8,128)(2,1)} async-done(((bf16[8,128,2048]{2,1,0:T(8,128)(2,1)}), bf16[8,128,2048]{2,1,0:T(8,128)(2,1)}, u32[]{:S(2)}, u32[]{:S(2)}) %all-to-all-start) | async-done | bytes 4194336 | tf_op jit(solution)/shard_map/all_to_all | solution.py:58
  234.9 5.6 fusion.12
  240.5 6.4 fusion.36
  247.0 3.9 convolution_convert_fusion.1
  250.8 1.3 convolution_bitcast_fusion.1
  252.2 1.3 convolution_bitcast_fusion.2
  253.5 5.5 convolution_bitcast_fusion
  258.9 3.3 pad_maximum_fusion
  262.4 54.6 %all-reduce.6.cloned.1.call-done = f32[2,3,384,256]{3,2,0,1:T(8,128)} async-done(((f32[2,3,384,256]{3,2,0,1:T(8,128)}), f32[2,3,384,256]{3,2,0,1:T(8,128)}) %all-reduce.6.cloned.1.call-update) | async-done | bytes 2359312 | tf_op jit(solution)/shard_map/psum | solution.py:111
  317.0 2.9 convert_element_type.71
  319.9 5.4 fusion.20
  325.3 2.7 fusion.52
  328.0 6.5 fusion.26
  334.5 4.6 fusion.14
  339.1 2.4 fusion.1
  341.5 2.8 copy.24
  344.4 5.5 all-to-all-start.2
  349.9 3.4 copy.30
  353.3 191.2 %all-to-all-done.2 = bf16[8,128,2048]{2,1,0:T(8,128)(2,1)} async-done(((bf16[8,128,2048]{2,1,0:T(8,128)(2,1)}), bf16[8,128,2048]{2,1,0:T(8,128)(2,1)}, u32[]{:S(2)}, u32[]{:S(2)}) %all-to-all-start.2) | async-done | bytes 4194336 | tf_op jit(solution)/shard_map/all_to_all | solution.py:93
  544.5 4.8 concatenate.18
  549.3 11.6 %gather_fusion.3 = bf16[1024,2048]{1,0:T(8,128)(2,1)} fusion(bf16[1025,2048]{1,0:T(8,128)(2,1)} %concatenate.18, s32[1024]{0:T(1024)S(1)} %broadcast_clamp_fusion), kind=kCustom, calls=%fused_computation.3 | custom fusion | bytes 8392704 | tf_op jit(solution)/shard_map/gather | solution.py:98
  560.9 5.9 bitcast_reduce_fusion
  566.8 203.9 %all-gather.6.cloned.1.call-done = f32[65536,256]{1,0:T(8,128)} async-done(((f32[2048,256]{1,0:T(8,128)}), f32[65536,256]{1,0:T(8,128)}) %all-gather.6.cloned.1.call-update) | async-done | bytes 67108880 | tf_op jit(solution)/shard_map/all_gather | solution.py:10
  770.8 22.4 %reduce_sum.22 = f32[2048,256]{1,0:T(8,128)} reduce(f32[32,2048,256]{2,1,0:T(8,128)} %bitcast.47, f32[]{:T(128)} %constant.119.clone.1), dimensions={0}, to_apply=%region_3.4 | reduce | flops 16252928 | bytes 69206016 | tf_op jit(solution)/shard_map/reduce_sum | solution.py:10
  793.1 5.7 fusion.72
  801.4 11.7 %cholesky.50 = f32[128,128]{1,0:T(8,128)S(1)} custom-call(f32[128,128]{1,0:T(8,128)S(1)} %cholesky.118), custom_call_target="Cholesky" | custom-call | tf_op jit(solution)/shard_map/jit(cholesky)/cholesky | solution.py:135
  813.1 1.7 dynamic-slice_bitcast_fusion
  814.8 9.8 %custom-call.15 = f32[1,128,128]{1,2,0:T(8,128)S(1)} custom-call(f32[1,128,128]{2,1,0:T(8,128)S(1)} %get-tuple-element.33), custom_call_target="InvertDiagBlocksLowerTriangular" | custom-call | tf_op jit(solution)/shard_map/jit(cholesky)/cholesky | solution.py:135
  824.6 1.0 constant_dynamic-update-slice_fusion.1
  825.7 1.1 convolution_subtract_fusion.1
  826.8 12.0 %cholesky.105 = f32[128,128]{1,0:T(8,128)S(1)} custom-call(f32[128,128]{1,0:T(8,128)S(1)} %convolution_subtract_fusion.1), custom_call_target="Cholesky" | custom-call | tf_op jit(solution)/shard_map/jit(cholesky)/cholesky | solution.py:135
  841.8 5.2 while.1
  842.4 2.0 bitcast_dynamic-update-slice_fusion.2
  845.0 2.0 bitcast_dynamic-update-slice_fusion.2
  847.0 20.5 %custom-call.16 = f32[2,128,128]{1,2,0:T(8,128)S(1)} custom-call(f32[2,128,128]{2,1,0:T(8,128)} %get-tuple-element.10), custom_call_target="InvertDiagBlocksLowerTriangular" | custom-call | tf_op jit(solution)/shard_map/jit(_solve_triangular)/triangular_solve | solution.py:137
  867.5 1.2 fusion.55
  868.7 1.3 convolution_subtract_fusion
  (54 shorter events, 9.7 us)
Async XLA Ops:
  7.2 233.4 %copy-start = (bf16[2,2048,384]{2,1,0:T(8,128)(2,1)S(1)}, bf16[2,2048,384]{2,1,0:T(8,128)(2,1)}, u32[]{:S(2)}) copy-start(bf16[2,2048,384]{2,1,0:T(8,128)(2,1)} %param.17) | copy-start | bytes 9437188
  24.5 100.6 %all-to-all-start.1 = ((bf16[8,128,2048]{2,1,0:T(8,128)(2,1)}), bf16[8,128,2048]{2,1,0:T(8,128)(2,1)}, u32[]{:S(2)}, u32[]{:S(2)}) async-start(bf16[8,128,2048]{2,1,0:T(8,128)(2,1)} %bitcast.179), calls=%async_computation.1 | async-start | bytes 8388608 | tf_op jit(solution)/shard_map/all_to_all | solution.py:57
  33.7 10.0 %copy-start.7 = (f32[128,8]{0,1:T(8,128)S(1)}, f32[128,8]{0,1:T(8,128)}, u32[]{:S(2)}) copy-start(f32[128,8]{0,1:T(8,128)} %param.12) | copy-start | bytes 12292
  54.9 74.8 %copy-start.6 = (f32[256,256]{1,0:T(8,128)S(1)}, f32[256,256]{1,0:T(8,128)}, u32[]{:S(2)}) copy-start(f32[256,256]{1,0:T(8,128)} %param.19) | copy-start | bytes 786436
  125.1 109.8 %all-to-all-start = ((bf16[8,128,2048]{2,1,0:T(8,128)(2,1)}), bf16[8,128,2048]{2,1,0:T(8,128)(2,1)}, u32[]{:S(2)}, u32[]{:S(2)}) async-start(bf16[8,128,2048]{2,1,0:T(8,128)(2,1)} %fusion), calls=%async_computation | async-start | bytes 8388608 | tf_op jit(solution)/shard_map/all_to_all | solution.py:58
  129.7 117.3 %all-gather.4.cloned.1.call-start = ((), (), s32[]{:S(2)}) async-start(), calls=%async_computation.3 | async-start | bytes 1179648 | tf_op jit(solution)/shard_map/all_gather | solution.py:51
  130.4 186.6 %all-reduce.6.cloned.1.call-start = ((), (), s32[]{:S(2)}) async-start(), calls=%async_computation.4 | async-start | bytes 4718592 | tf_op jit(solution)/shard_map/psum | solution.py:111
  234.9 5.6 copy-start.8
  246.9 3.9 copy-start.4
  246.9 5.2 copy-start.1
  262.2 508.5 %all-gather.6.cloned.1.call-start = ((), (), s32[]{:S(2)}) async-start(), calls=%async_computation.5 | async-start | bytes 69206016 | tf_op jit(solution)/shard_map/all_gather | solution.py:10
  334.5 4.6 copy-start.5
  344.4 200.1 %all-to-all-start.2 = ((bf16[8,128,2048]{2,1,0:T(8,128)(2,1)}), bf16[8,128,2048]{2,1,0:T(8,128)(2,1)}, u32[]{:S(2)}, u32[]{:S(2)}) async-start(bf16[8,128,2048]{2,1,0:T(8,128)(2,1)} %bitcast.181), calls=%async_computation.2 | async-start | bytes 8388608 | tf_op jit(solution)/shard_map/all_to_all | solution.py:93
  800.6 0.7 copy-start.3
  838.8 2.0 copy-start.2
Sparse Core Ops, SparseCore 0:
  133.2 102.2 all-gather.3
  262.3 54.6 all-reduce.5
  334.6 436.0 all-gather.5
